TPU v7x, 32 devices: a whole 2x2x4 slice. The times are simulated.
32 devices in a mesh: tiles: 16 (over z, y, x), depth: 2 (over core).
Axes of the slice: x: 2, y: 2, z: 4, core: 2. Of those that a mesh axis runs over, the one named last changes fastest.
Arguments:
- momentum: float32 [16, 16, 6300], P('tiles', 'depth'), may hold values from -6 to 6
- tracer: float32 [16, 16, 6300], P('tiles', 'depth'), may hold values from -6 to 6
- mom_diffusivity: float32 [16, 16, 6300], P('tiles', 'depth'), may hold values from 0.02 to 0.2
- tra_diffusivity: float32 [16, 16, 6300], P('tiles', 'depth'), may hold values from 0.02 to 0.2
- mixing: float32 [16, 16, 6300], P('tiles', 'depth'), may hold values from 0.05 to 0.4
- wet_mask: int32 [16, 6300], P('tiles'), may hold values 0 or 1
- neighbours: int32 [16, 4], P('tiles'), may hold values from -1 to 15, as said below
- source_edges: int32 [16, 4], P('tiles'), may hold values from 0 to 3, as said below
- flips: int32 [16, 4], P('tiles'), may hold values from 0 to 1
- mom_cotangent: float32 [16, 16, 6300], P('tiles', 'depth'), may hold values from -6 to 6
- tra_cotangent: float32 [16, 16, 6300], P('tiles', 'depth'), may hold values from -6 to 6
Outputs:
- final_momentum: float32 [16, 16, 6300], P('tiles', 'depth')
- final_tracer: float32 [16, 16, 6300], P('tiles', 'depth')
- grad_momentum: float32 [16, 16, 6300], P('tiles', 'depth')
- grad_tracer: float32 [16, 16, 6300], P('tiles', 'depth')
Inputs may be any that keep to these rules, and one draw needn't show every extreme that they name: `neighbours`: the neighbour relation is symmetric, also across the fold seam, where a tile's north edge faces another tile's north edge in reverse order; -1 marks a missing neighbour. `source_edges`: for north and south directions the facing edge is north or south, for east and west directions it is east or west.
All inputs are finite; a program needn't handle non-finite values. No bound on the sum of `wet_mask` on one device may be relied on, other than what follows from the above.
Results may differ from a plain program's by a relative error of at most 0.00002.
Values sent between devices are 32-bit elements; how exact they have to be, the bound alone decides.
A program may use at most 64 MiB of HBM per device.

v0:
```python
import jax
import jax.numpy as jnp
from jax import lax
from jax.sharding import PartitionSpec as P

NI = 90
NJ = 70


def padded_2(block, sides, width):
    for axis, dim in sides:
        count = lax.axis_size(axis)
        forward = [(i, i + 1) for i in range(count - 1)]
        backward = [(target, source) for source, target in forward]
        low = lax.ppermute(
            lax.slice_in_dim(block, block.shape[dim] - width, None, axis=dim), axis, forward
        )
        high = lax.ppermute(lax.slice_in_dim(block, 0, width, axis=dim), axis, backward)
        block = jnp.concatenate([low, block, high], axis=dim)
    return block


def carried_in(part, axis, combine, identity, reverse):
    count = lax.axis_size(axis)
    place = lax.axis_index(axis)
    ahead = count - 1 - place if reverse else place
    gathered = lax.all_gather(part, axis)
    state = jnp.zeros_like(part) + jnp.asarray(identity, part.dtype)

    def one(hop, state):
        source = count - 1 - hop if reverse else hop
        return combine(state, lax.dynamic_index_in_dim(gathered, source, 0, False))

    return lax.fori_loop(0, ahead, one, state)


def edges_of(field):
    total = field.shape[-1]
    return jnp.concatenate(
        [field[..., total - NI :], field[..., :NI], field[..., NI - 1 :: NI], field[..., ::NI]],
        axis=-1,
    )


def pick_edge(chosen, source, flip, direction):
    if direction < 2:
        strip = jnp.where(source[:, None, None] == 0, chosen[..., :NI], chosen[..., NI : 2 * NI])
    else:
        strip = jnp.where(
            source[:, None, None] == 2,
            chosen[..., 2 * NI : 2 * NI + NJ],
            chosen[..., 2 * NI + NJ :],
        )
    return jnp.where(flip[:, None, None] == 1, strip[..., ::-1], strip)


def select_strips(neighbours, source_edges, flips, carry, pieces):
    spans = [(0, NI), (NI, NI), (2 * NI, NJ), (2 * NI + NJ, NJ)]
    results = []
    for held, piece in zip(carry, pieces):
        count = piece.shape[0]
        strips = []
        for direction in range(4):
            target = neighbours[:, direction]
            valid = (target >= 0) & (target < count)
            row_index = jnp.clip(target, 0, count - 1)
            chosen = jnp.take(piece, row_index, axis=0)
            strip = pick_edge(chosen, source_edges[:, direction], flips[:, direction], direction)
            offset, length = spans[direction]
            strips.append(
                jnp.where(valid[:, None, None], strip, held[..., offset : offset + length])
            )
        results.append(jnp.concatenate(strips, axis=-1))
    return tuple(results)


def shifted_sum(values, halo):
    total = values.shape[-1]
    column = jnp.arange(total) % NI
    north = jnp.concatenate([values[..., NI:], halo[..., :NI]], axis=-1)
    south = jnp.concatenate([halo[..., NI : 2 * NI], values[..., : total - NI]], axis=-1)
    east_halo = jnp.repeat(halo[..., 2 * NI : 2 * NI + NJ], NI, axis=-1)
    west_halo = jnp.repeat(halo[..., 2 * NI + NJ :], NI, axis=-1)
    east = jnp.where(
        column == NI - 1, east_halo, jnp.concatenate([values[..., 1:], values[..., :1]], axis=-1)
    )
    west = jnp.where(
        column == 0, west_halo, jnp.concatenate([values[..., -1:], values[..., :-1]], axis=-1)
    )
    return north + south + east + west


def laplace(field, weighted_halo, wet, wet_halo):
    values = shifted_sum(wet * field, weighted_halo)
    weights = shifted_sum(wet, wet_halo)
    return wet * (values - weights * field)


def add_one(earlier, later):
    return earlier + later


def local(
    momentum,
    tracer,
    mom_diffusivity,
    tra_diffusivity,
    mixing,
    wet_mask,
    neighbours,
    source_edges,
    flips,
    mom_cotangent,
    tra_cotangent,
):
    slot_count = momentum.shape[0]
    level_count = momentum.shape[1]
    edge_cells = 2 * NI + 2 * NJ
    depth_count = lax.axis_size("depth")
    depth_index = lax.axis_index("depth")
    levels_all = level_count * depth_count
    press_scale = levels_all ** (-0.5)
    level_index = depth_index * level_count + jnp.arange(level_count)
    has_above = (level_index > 0).astype(jnp.float32)[None, :, None]
    has_below = (level_index < levels_all - 1).astype(jnp.float32)[None, :, None]

    def fold_strips(carry, pieces):
        return select_strips(neighbours, source_edges, flips, carry, pieces)

    mask_start = jnp.zeros((slot_count, 1, edge_cells), jnp.int32)
    wet_halo = fold_strips(
        (mask_start,),
        (lax.all_gather(edges_of(wet_mask[:, None, :]), "tiles", axis=0, tiled=True),),
    )[0]
    wet_halo = wet_halo.astype(jnp.float32)
    wet = wet_mask[:, None, :].astype(jnp.float32)
    zeros_edge = jnp.zeros((slot_count, level_count, edge_cells), jnp.float32)
    zeros_cells = jnp.zeros((slot_count, momentum.shape[2]), jnp.float32)

    def vertical_from(field, above, below):
        return has_above * (above - field) + has_below * (below - field)

    def level_halo(field):
        padded = padded_2(field, (("depth", 1),), 1)
        return (padded[:, :-2], padded[:, 2:])

    mom_now, tra_now = (momentum, tracer)
    for iteration in range(2):
        own_sum = jnp.cumsum(tra_now, axis=1)
        above, below = level_halo(tra_now)
        prior_own = carried_in(own_sum[:, -1], "depth", add_one, zeros_cells, False)
        press = press_scale * (own_sum + prior_own[:, None, :])
        mom_halo, tra_halo, press_halo = fold_strips(
            (zeros_edge, zeros_edge, zeros_edge),
            (
                lax.all_gather(edges_of(mom_now), "tiles", axis=0, tiled=True),
                lax.all_gather(edges_of(tra_now), "tiles", axis=0, tiled=True),
                lax.all_gather(edges_of(press), "tiles", axis=0, tiled=True),
            ),
        )
        mom_next = (
            mom_now
            + mom_diffusivity * laplace(mom_now, wet_halo * mom_halo, wet, wet_halo)
            - 0.1 * laplace(press, wet_halo * press_halo, wet, wet_halo)
        )
        tra_next = (
            tra_now
            + tra_diffusivity * laplace(tra_now, wet_halo * tra_halo, wet, wet_halo)
            + mixing * vertical_from(tra_now, above, below)
            + 0.2 * mom_now
        )
        mom_now, tra_now = (mom_next, tra_next)
    mom_adjoint, tra_adjoint = (mom_cotangent, tra_cotangent)
    for iteration in range(2):
        mom_weighted = mom_diffusivity * mom_adjoint
        tra_weighted = tra_diffusivity * tra_adjoint
        cycle_mom, cycle_plain, cycle_tra = fold_strips(
            (zeros_edge, zeros_edge, zeros_edge),
            (
                lax.all_gather(edges_of(wet * mom_weighted), "tiles", axis=0, tiled=True),
                lax.all_gather(edges_of(wet * mom_adjoint), "tiles", axis=0, tiled=True),
                lax.all_gather(edges_of(wet * tra_weighted), "tiles", axis=0, tiled=True),
            ),
        )
        press_adjoint = -0.1 * laplace(mom_adjoint, cycle_plain, wet, wet_halo)
        mixed = mixing * tra_adjoint
        later_sum = jnp.flip(jnp.cumsum(jnp.flip(press_adjoint, axis=1), axis=1), axis=1)
        after = carried_in(later_sum[:, 0], "depth", add_one, zeros_cells, True)
        above, below = level_halo(mixed)
        press_back = press_scale * (later_sum + after[:, None, :])
        mom_back = mom_adjoint + laplace(mom_weighted, cycle_mom, wet, wet_halo) + 0.2 * tra_adjoint
        tra_back = (
            tra_adjoint
            + laplace(tra_weighted, cycle_tra, wet, wet_halo)
            + vertical_from(mixed, above, below)
            + press_back
        )
        mom_adjoint, tra_adjoint = (mom_back, tra_back)
    return (mom_now, tra_now, mom_adjoint, tra_adjoint)


def solution(mesh):
    in_specs = (
        P("tiles", "depth", None),
        P("tiles", "depth", None),
        P("tiles", "depth", None),
        P("tiles", "depth", None),
        P("tiles", "depth", None),
        P("tiles", None),
        P("tiles", None),
        P("tiles", None),
        P("tiles", None),
        P("tiles", "depth", None),
        P("tiles", "depth", None),
    )
    out_specs = (
        P("tiles", "depth", None),
        P("tiles", "depth", None),
        P("tiles", "depth", None),
        P("tiles", "depth", None),
    )
    return jax.shard_map(local, mesh=mesh, in_specs=in_specs, out_specs=out_specs, check_vma=False)
```

profile of v0, /device:TPU:0, one launch (start us, length us, event | category | flops | bytes accessed | tf_op | source)
XLA Modules:
  0.0 668.3 jit_solution(13493256316628074655)
XLA Ops:
  1.5 1.1 broadcast_multiply_fusion.6
  19.5 42.5 %all_gather.51 = s32[16,1,320]{2,1,0:T(1,128)S(1)} all-gather(s32[1,1,320]{2,1,0:T(1,128)S(1)} %pad_add_fusion), channel_id=1, replica_groups=mesh['tiles'=16,'depth'=2] {'tiles'}, dimensions={0}, use_global_device_ids=true | all-gather | bytes 21760 | tf_op jit(solution)/shard_map/all_gather | solution.py:133
  65.6 36.5 %all_gather.60 = f32[16,8,320]{2,1,0:T(8,128)S(1)} all-gather(f32[1,8,320]{2,1,0:T(8,128)S(1)} %pad_maximum_fusion.14), channel_id=1, replica_groups=mesh['tiles'=16,'depth'=2] {'tiles'}, dimensions={0}, use_global_device_ids=true | all-gather | bytes 174080 | tf_op jit(solution)/shard_map/all_gather | solution.py:180
  103.1 38.7 %all_gather.56 = f32[16,8,320]{2,1,0:T(8,128)S(1)} all-gather(f32[1,8,320]{2,1,0:T(8,128)S(1)} %pad_maximum_fusion.11), channel_id=1, replica_groups=mesh['tiles'=16,'depth'=2] {'tiles'}, dimensions={0}, use_global_device_ids=true | all-gather | bytes 174080 | tf_op jit(solution)/shard_map/all_gather | solution.py:157
  144.7 2.0 broadcast_multiply_fusion.12
  146.7 1.0 broadcast_multiply_fusion.8
  148.3 1.9 collective-permute-start.4
  150.2 1.3 collective-permute-start.5
  152.2 4.2 collective-permute-start
  156.4 1.3 collective-permute-start.1
  164.3 0.8 fusion.166
  167.8 36.6 %all_gather.66 = f32[16,8,320]{2,1,0:T(8,128)S(1)} all-gather(f32[1,8,320]{2,1,0:T(8,128)S(1)} %pad_maximum_fusion.19), channel_id=1, replica_groups=mesh['tiles'=16,'depth'=2] {'tiles'}, dimensions={0}, use_global_device_ids=true | all-gather | bytes 174080 | tf_op jit(solution)/shard_map/all_gather | solution.py:181
  205.3 0.8 broadcast_in_dim.974
  207.8 1.3 fusion.95
  211.4 0.8 fusion.177
  212.8 38.4 %all_gather.52 = f32[16,8,320]{2,1,0:T(8,128)S(1)} all-gather(f32[1,8,320]{2,1,0:T(8,128)S(1)} %pad_maximum_fusion.8), channel_id=1, replica_groups=mesh['tiles'=16,'depth'=2] {'tiles'}, dimensions={0}, use_global_device_ids=true | all-gather | bytes 174080 | tf_op jit(solution)/shard_map/all_gather | solution.py:156
  259.5 36.6 %all_gather.62 = f32[16,8,320]{2,1,0:T(8,128)S(1)} all-gather(f32[1,8,320]{2,1,0:T(8,128)S(1)} %pad_maximum_fusion.16), channel_id=1, replica_groups=mesh['tiles'=16,'depth'=2] {'tiles'}, dimensions={0}, use_global_device_ids=true | all-gather | bytes 174080 | tf_op jit(solution)/shard_map/all_gather | solution.py:182
  297.8 38.4 %all_gather.63 = f32[16,8,320]{2,1,0:T(8,128)S(1)} all-gather(f32[1,8,320]{2,1,0:T(8,128)S(1)} %pad_maximum_fusion.17), channel_id=1, replica_groups=mesh['tiles'=16,'depth'=2] {'tiles'}, dimensions={0}, use_global_device_ids=true | all-gather | bytes 174080 | tf_op jit(solution)/shard_map/all_gather | solution.py:181
  336.5 0.8 broadcast_in_dim.968
  337.7 0.8 broadcast_in_dim.966
  339.7 1.5 fusion.86
  342.2 1.8 all_gather.64
  345.0 36.6 %all_gather.61 = f32[16,8,320]{2,1,0:T(8,128)S(1)} all-gather(f32[1,8,320]{2,1,0:T(8,128)S(1)} %pad_maximum_fusion.15), channel_id=1, replica_groups=mesh['tiles'=16,'depth'=2] {'tiles'}, dimensions={0}, use_global_device_ids=true | all-gather | bytes 174080 | tf_op jit(solution)/shard_map/all_gather | solution.py:180
  383.4 1.8 all_gather.67
  385.6 1.8 all_gather.53
  389.1 14.9 %rev.214 = f32[1,8,6300]{2,1,0:T(8,128)} reverse(f32[1,8,6300]{2,1,0:T(8,128)S(1)} %reduce_window_sum.27), dimensions={1} | reverse | bytes 403200 | tf_op jit(solution)/shard_map/jit(_flip)/rev | solution.py:187
  404.8 0.8 broadcast_in_dim.962
  405.8 0.8 broadcast_in_dim.964
  406.7 0.8 broadcast_in_dim.958
  407.7 0.8 broadcast_in_dim.960
  409.4 0.8 broadcast_in_dim.942
  410.4 0.8 broadcast_in_dim.944
  412.6 1.7 broadcast_multiply_fusion.2
  416.5 1.0 fusion.165
  421.3 1.5 broadcast_multiply_fusion.7
  423.3 1.8 all_gather.57
  426.8 1.1 slice.1238
  427.9 1.1 slice.1239
  429.4 38.4 %all_gather.59 = f32[16,8,320]{2,1,0:T(8,128)S(1)} all-gather(f32[1,8,320]{2,1,0:T(8,128)S(1)} %pad_maximum_fusion.13), channel_id=1, replica_groups=mesh['tiles'=16,'depth'=2] {'tiles'}, dimensions={0}, use_global_device_ids=true | all-gather | bytes 174080 | tf_op jit(solution)/shard_map/all_gather | solution.py:157
  468.8 36.7 %all_gather.54 = f32[16,8,320]{2,1,0:T(8,128)S(1)} all-gather(f32[1,8,320]{2,1,0:T(8,128)S(1)} %pad_maximum_fusion.9), channel_id=1, replica_groups=mesh['tiles'=16,'depth'=2] {'tiles'}, dimensions={0}, use_global_device_ids=true | all-gather | bytes 174080 | tf_op jit(solution)/shard_map/all_gather | solution.py:158
  506.5 38.4 %all_gather.58 = f32[16,8,320]{2,1,0:T(8,128)S(1)} all-gather(f32[1,8,320]{2,1,0:T(8,128)S(1)} %pad_maximum_fusion.12), channel_id=1, replica_groups=mesh['tiles'=16,'depth'=2] {'tiles'}, dimensions={0}, use_global_device_ids=true | all-gather | bytes 174080 | tf_op jit(solution)/shard_map/all_gather | solution.py:158
  551.8 0.8 fusion.201
  556.4 36.8 %all_gather.65 = f32[16,8,320]{2,1,0:T(8,128)S(1)} all-gather(f32[1,8,320]{2,1,0:T(8,128)S(1)} %pad_maximum_fusion.18), channel_id=1, replica_groups=mesh['tiles'=16,'depth'=2] {'tiles'}, dimensions={0}, use_global_device_ids=true | all-gather | bytes 174080 | tf_op jit(solution)/shard_map/all_gather | solution.py:182
  595.2 1.9 collective-permute-start.2
  597.1 1.3 collective-permute-start.3
  599.2 0.8 broadcast_in_dim.972
  600.1 0.8 broadcast_in_dim.970
  601.0 4.2 collective-permute-start.6
  605.2 1.3 collective-permute-start.7
  606.6 0.8 broadcast_in_dim.924
  607.6 0.8 broadcast_in_dim.927
  608.5 0.8 broadcast_in_dim.934
  609.5 0.8 broadcast_in_dim.936
  610.5 0.8 broadcast_in_dim.950
  611.4 0.8 broadcast_in_dim.952
  612.4 0.8 broadcast_in_dim.946
  613.4 0.8 broadcast_in_dim.948
  615.0 3.4 fusion.19
  619.0 0.8 fusion.189
  619.9 38.2 %all_gather.55 = f32[16,8,320]{2,1,0:T(8,128)S(1)} all-gather(f32[1,8,320]{2,1,0:T(8,128)S(1)} %pad_maximum_fusion.10), channel_id=1, replica_groups=mesh['tiles'=16,'depth'=2] {'tiles'}, dimensions={0}, use_global_device_ids=true | all-gather | bytes 174080 | tf_op jit(solution)/shard_map/all_gather | solution.py:156
  660.6 0.8 broadcast_in_dim.938
  661.5 0.8 broadcast_in_dim.940
  663.1 2.7 fusion.48
  666.5 1.7 fusion.4
  (537 shorter events, 79.5 us)
Async XLA Ops:
  1.4 7.8 %copy-start.3 = (f32[1,8,6300]{2,1,0:T(8,128)S(1)}, f32[1,8,6300]{2,1,0:T(8,128)}, u32[]{:S(2)}) copy-start(f32[1,8,6300]{2,1,0:T(8,128)} %param.24) | copy-start | bytes 604804
  6.6 5.6 copy-start.23
  102.7 43.9 %copy-start.6 = (f32[1,8,6300]{2,1,0:T(8,128)S(1)}, f32[1,8,6300]{2,1,0:T(8,128)}, u32[]{:S(2)}) copy-start(f32[1,8,6300]{2,1,0:T(8,128)} %param.33) | copy-start | bytes 604804
  103.1 43.5 %copy-start.5 = (f32[1,8,6300]{2,1,0:T(8,128)S(1)}, f32[1,8,6300]{2,1,0:T(8,128)}, u32[]{:S(2)}) copy-start(f32[1,8,6300]{2,1,0:T(8,128)} %param.32) | copy-start | bytes 604804
  142.4 4.2 copy-start.2
  143.1 3.6 copy-start.1
  143.2 3.5 copy-start
  148.3 263.5 %collective-permute-start.4 = (f32[1,1,6300]{2,1,0:T(1,128)}, f32[1,1,6300]{2,1,0:T(1,128)}, u32[]{:S(2)}, u32[]{:S(2)}) collective-permute-start(f32[1,1,6300]{2,1,0:T(1,128)} %get-tuple-element.272), channel_id=1, source_target_pairs={{0,1},{2,3},{4,5},{6,7},{8,9},{10,11},{12,13},{14,15},{16,17},{18,... | collective-permute-start | bytes 75608 | tf_op jit(solution)/shard_map/ppermute | solution.py:15
  150.2 261.7 %collective-permute-start.5 = (f32[1,1,6300]{2,1,0:T(1,128)}, f32[1,1,6300]{2,1,0:T(1,128)}, u32[]{:S(2)}, u32[]{:S(2)}) collective-permute-start(f32[1,1,6300]{2,1,0:T(1,128)} %get-tuple-element.273), channel_id=1, source_target_pairs={{1,0},{3,2},{5,4},{7,6},{9,8},{11,10},{13,12},{15,14},{17,16},{19,... | collective-permute-start | bytes 75608 | tf_op jit(solution)/shard_map/ppermute | solution.py:18
  152.2 268.4 %collective-permute-start = (f32[1,1,6300]{2,1,0:T(1,128)}, f32[1,1,6300]{2,1,0:T(1,128)}, u32[]{:S(2)}, u32[]{:S(2)}) collective-permute-start(f32[1,1,6300]{2,1,0:T(1,128)} %get-tuple-element.349), channel_id=1, source_target_pairs={{0,1},{2,3},{4,5},{6,7},{8,9},{10,11},{12,13},{14,15},{16,17},{18,... | collective-permute-start | bytes 75608 | tf_op jit(solution)/shard_map/ppermute | solution.py:15
  156.4 264.2 %collective-permute-start.1 = (f32[1,1,6300]{2,1,0:T(1,128)}, f32[1,1,6300]{2,1,0:T(1,128)}, u32[]{:S(2)}, u32[]{:S(2)}) collective-permute-start(f32[1,1,6300]{2,1,0:T(1,128)} %get-tuple-element.350), channel_id=1, source_target_pairs={{1,0},{3,2},{5,4},{7,6},{9,8},{11,10},{13,12},{15,14},{17,16},{19,... | collective-permute-start | bytes 75608 | tf_op jit(solution)/shard_map/ppermute | solution.py:18
  205.3 1.9 copy-start.4
  251.2 3.1 copy-start.95
  251.2 0.7 copy-start.25
  252.0 0.7 copy-start.24
  255.0 0.7 copy-start.57
  258.7 0.7 copy-start.76
  296.9 0.7 copy-start.65
  296.9 0.7 copy-start.66
  296.9 0.7 copy-start.73
  296.9 0.8 copy-start.74
  337.7 1.3 copy-start.12
  389.1 22.8 %copy-start.77 = (f32[8]{0:T(128)}, f32[8]{0:T(128)S(1)}, u32[]{:S(2)}) copy-start(f32[8]{0:T(128)S(1)} %get-tuple-element.455) | copy-start | bytes 100
  389.1 22.8 %copy-start.81 = (f32[8]{0:T(128)}, f32[8]{0:T(128)S(1)}, u32[]{:S(2)}) copy-start(f32[8]{0:T(128)S(1)} %get-tuple-element.456) | copy-start | bytes 100
  415.0 1.5 copy-start.10
  415.0 1.5 copy-start.11
  415.0 1.5 copy-start.16
  415.0 1.5 copy-start.17
  417.6 3.0 copy-start.9
  420.6 0.7 copy-start.35
  425.2 0.7 copy-start.22
  425.2 0.8 copy-start.19
  545.6 0.7 copy-start.55
  545.6 0.7 copy-start.56
  545.6 0.7 copy-start.59
  545.6 0.7 copy-start.60
  555.6 0.7 copy-start.62
  555.6 0.7 copy-start.69
  555.6 0.7 copy-start.70
  595.2 19.0 %collective-permute-start.2 = (f32[1,1,6300]{2,1,0:T(1,128)}, f32[1,1,6300]{2,1,0:T(1,128)}, u32[]{:S(2)}, u32[]{:S(2)}) collective-permute-start(f32[1,1,6300]{2,1,0:T(1,128)} %get-tuple-element.339), channel_id=1, source_target_pairs={{0,1},{2,3},{4,5},{6,7},{8,9},{10,11},{12,13},{14,15},{16,17},{18,... | collective-permute-start | bytes 75608 | tf_op jit(solution)/shard_map/ppermute | solution.py:15
  597.1 17.2 %collective-permute-start.3 = (f32[1,1,6300]{2,1,0:T(1,128)}, f32[1,1,6300]{2,1,0:T(1,128)}, u32[]{:S(2)}, u32[]{:S(2)}) collective-permute-start(f32[1,1,6300]{2,1,0:T(1,128)} %get-tuple-element.340), channel_id=1, source_target_pairs={{1,0},{3,2},{5,4},{7,6},{9,8},{11,10},{13,12},{15,14},{17,16},{19,... | collective-permute-start | bytes 75608 | tf_op jit(solution)/shard_map/ppermute | solution.py:18
  601.0 64.8 %collective-permute-start.6 = (f32[1,1,6300]{2,1,0:T(1,128)}, f32[1,1,6300]{2,1,0:T(1,128)}, u32[]{:S(2)}, u32[]{:S(2)}) collective-permute-start(f32[1,1,6300]{2,1,0:T(1,128)} %get-tuple-element.260), channel_id=1, source_target_pairs={{0,1},{2,3},{4,5},{6,7},{8,9},{10,11},{12,13},{14,15},{16,17},{18,... | collective-permute-start | bytes 75608 | tf_op jit(solution)/shard_map/ppermute | solution.py:15
  605.2 60.6 %collective-permute-start.7 = (f32[1,1,6300]{2,1,0:T(1,128)}, f32[1,1,6300]{2,1,0:T(1,128)}, u32[]{:S(2)}, u32[]{:S(2)}) collective-permute-start(f32[1,1,6300]{2,1,0:T(1,128)} %get-tuple-element.261), channel_id=1, source_target_pairs={{1,0},{3,2},{5,4},{7,6},{9,8},{11,10},{13,12},{15,14},{17,16},{19,... | collective-permute-start | bytes 75608 | tf_op jit(solution)/shard_map/ppermute | solution.py:18
  613.4 0.9 copy-start.13
  613.4 0.9 copy-start.45
  613.4 0.9 copy-start.46
  613.4 0.9 copy-start.47
  614.2 0.8 copy-start.18
  614.2 0.8 copy-start.44
  614.3 0.7 copy-start.29
  614.3 0.7 copy-start.28
  614.3 0.7 copy-start.79
  614.3 0.7 copy-start.83
  661.5 0.9 copy-start.42
  662.4 0.7 copy-start.51
  662.4 0.7 copy-start.52
  662.4 0.7 copy-start.41
  663.1 2.8 copy-start.7
  663.1 2.8 copy-start.8
  663.1 2.8 copy-start.14
  663.1 2.8 copy-start.15
  663.1 2.8 copy-start.21
  663.1 2.8 copy-start.36
  663.1 2.8 copy-start.43
  (40 other events, 26.4 us)
where the time goes:
time: 670 us; the launch traced here: 668 us
  blocking collectives  500 us (75%)
  local copies, waits for them, and re-layouts  98.7 us (15%)
  other arithmetic  37 us (6%)
  starting transfers between devices  17.3 us (3%)
  between operations  15 us (2%)
    all_gather x2, blocking collectives, local(): lax.all_gather(edges_of(tra_now), 'tiles', axis=0, tiled=True)  77.1 us
    all_gather x2, blocking collectives, local(): lax.all_gather(edges_of(mom_now), 'tiles', axis=0, tiled=True)  76.6 us
    all_gather x2, blocking collectives, local(): lax.all_gather(edges_of(press), 'tiles', axis=0, tiled=True)  75 us
    all_gather x2, blocking collectives, local(): lax.all_gather(edges_of(wet * mom_adjoint), 'tiles', axis=0, tiled=True)  75 us
    all_gather x2, blocking collectives, local(): lax.all_gather(edges_of(wet * tra_weighted), 'tiles', axis=0, tiled=True)  73.4 us
    all_gather x2, blocking collectives, local(): lax.all_gather(edges_of(wet * mom_weighted), 'tiles', axis=0, tiled=True)  73.1 us
    all_gather x1, blocking collectives, local(): lax.all_gather(edges_of(wet_mask[:, None, :]), 'tiles', axis=0, tiled=True)  42.5 us
    rev x2, local copies, waits for them, and re-layouts, local(): jnp.flip(jnp.cumsum(jnp.flip(press_adjoint, axis=1), axis=1), axis=1)  15.6 us
  transfers between devices with their start and end apart: 8, of which 0 were waited for; matrix products, arithmetic and copies ran while one was open for 13% of the time, Pallas kernels for 0%

commit v1 on v0

--- a/solution.py
+++ b/solution.py
@@ -1,3 +1,4 @@
+import functools
 import jax
 import jax.numpy as jnp
 from jax import lax
@@ -5,6 +6,25 @@
 
 NI = 90
 NJ = 70
+
+
+def pages_answer(s0, peer_axis):
+    found_now = lax.axis_size(peer_axis)
+    a_next, z2, carry_out = (found_now, lax.axis_index(peer_axis), s0.shape[0])
+    z1, piece_out = (s0, 1)
+    while piece_out < a_next:
+        z1 = jnp.concatenate(
+            [
+                z1,
+                lax.ppermute(z1, peer_axis, [(b, (b - piece_out) % a_next) for b in range(a_next)]),
+            ],
+            axis=0,
+        )
+        piece_out = 2 * piece_out
+    return jnp.roll(z1, z2 * carry_out, axis=0)
+
+
+review_copies = functools.partial(pages_answer, peer_axis="tiles")
 
 
 def padded_2(block, sides, width):
@@ -153,7 +173,7 @@
         mom_halo, tra_halo, press_halo = fold_strips(
             (zeros_edge, zeros_edge, zeros_edge),
             (
-                lax.all_gather(edges_of(mom_now), "tiles", axis=0, tiled=True),
+                review_copies(edges_of(mom_now)),
                 lax.all_gather(edges_of(tra_now), "tiles", axis=0, tiled=True),
                 lax.all_gather(edges_of(press), "tiles", axis=0, tiled=True),
             ),

time: 670 us -> 627 us (0.936)
  blocking collectives: 500 us -> 426 us
  waiting for transfers between devices: 0.02 us -> 24.1 us
    all_gather x2 -> x0, blocking collectives: 76.6 us -> none  [local(): lax.all_gather(edges_of(mom_now), 'tiles', axis=0, tiled=True)]
    ppermute x0 -> x8, waiting for transfers between devices: none -> 24 us  [pages_answer(): lax.ppermute(z1, peer_axis, [(b, (b - piece_out) % a_next) for b in range...]
    unnamed x192 -> x258, local copies, waits for them, and re-layouts: 12.2 us -> 17.1 us
  transfers between devices with their start and end apart: 8 -> 16, of which waited for: 0 -> 6; matrix products, arithmetic and copies ran while one was open for 13% -> 14% of each run, Pallas kernels for 0% -> 0%
where the time goes in v1:
time: 627 us; the launch traced here: 622 us
  blocking collectives  426 us (68%)
  local copies, waits for them, and re-layouts  96.7 us (15%)
  other arithmetic  43.3 us (7%)
  waiting for transfers between devices  24.1 us (4%)
  starting transfers between devices  16.3 us (3%)
  between operations  15.6 us (2%)
    all_gather x2, blocking collectives, local(): lax.all_gather(edges_of(wet * mom_adjoint), 'tiles', axis=0, tiled=True)  76.4 us
    all_gather x2, blocking collectives, local(): lax.all_gather(edges_of(wet * tra_weighted), 'tiles', axis=0, tiled=True)  75.8 us
    all_gather x2, blocking collectives, local(): lax.all_gather(edges_of(tra_now), 'tiles', axis=0, tiled=True)  75.7 us
    all_gather x2, blocking collectives, local(): lax.all_gather(edges_of(press), 'tiles', axis=0, tiled=True)  75 us
    all_gather x2, blocking collectives, local(): lax.all_gather(edges_of(wet * mom_weighted), 'tiles', axis=0, tiled=True)  73.4 us
    all_gather x1, blocking collectives, local(): lax.all_gather(edges_of(wet_mask[:, None, :]), 'tiles', axis=0, tiled=True)  42.5 us
    ppermute x8, waiting for transfers between devices, pages_answer(): lax.ppermute(z1, peer_axis, [(b, (b - piece_out) % a_next) for b in range...  24 us
    unnamed x258, local copies, waits for them, and re-layouts  17.1 us
  transfers between devices with their start and end apart: 16, of which 6 were waited for; matrix products, arithmetic and copies ran while one was open for 14% of the time, Pallas kernels for 0%

profile of v1, /device:TPU:0, one launch (start us, length us, event | category | flops | bytes accessed | tf_op | source)
XLA Modules:
  0.0 622.0 jit_solution(2764073047667400929)
XLA Ops:
  1.5 1.1 broadcast_multiply_fusion.6
  19.7 42.5 %all_gather.45 = s32[16,1,320]{2,1,0:T(1,128)S(1)} all-gather(s32[1,1,320]{2,1,0:T(1,128)S(1)} %pad_add_fusion), channel_id=1, replica_groups=mesh['tiles'=16,'depth'=2] {'tiles'}, dimensions={0}, use_global_device_ids=true | all-gather | bytes 21760 | tf_op jit(solution)/shard_map/all_gather | solution.py:153
  66.4 36.5 %all_gather.52 = f32[16,8,320]{2,1,0:T(8,128)S(1)} all-gather(f32[1,8,320]{2,1,0:T(8,128)S(1)} %pad_maximum_fusion.20), channel_id=1, replica_groups=mesh['tiles'=16,'depth'=2] {'tiles'}, dimensions={0}, use_global_device_ids=true | all-gather | bytes 174080 | tf_op jit(solution)/shard_map/all_gather | solution.py:200
  104.0 38.7 %all_gather.48 = f32[16,8,320]{2,1,0:T(8,128)S(1)} all-gather(f32[1,8,320]{2,1,0:T(8,128)S(1)} %pad_maximum_fusion.17), channel_id=1, replica_groups=mesh['tiles'=16,'depth'=2] {'tiles'}, dimensions={0}, use_global_device_ids=true | all-gather | bytes 174080 | tf_op jit(solution)/shard_map/all_gather | solution.py:177
  145.5 2.0 broadcast_multiply_fusion.12
  147.5 1.3 broadcast_multiply_fusion.8
  149.5 1.9 collective-permute-start.12
  151.4 1.3 collective-permute-start.13
  154.8 4.2 collective-permute-start.8
  159.0 1.3 collective-permute-start.9
  168.9 0.8 fusion.166
  170.5 38.3 %all_gather.58 = f32[16,8,320]{2,1,0:T(8,128)S(1)} all-gather(f32[1,8,320]{2,1,0:T(8,128)S(1)} %pad_maximum_fusion.25), channel_id=1, replica_groups=mesh['tiles'=16,'depth'=2] {'tiles'}, dimensions={0}, use_global_device_ids=true | all-gather | bytes 174080 | tf_op jit(solution)/shard_map/all_gather | solution.py:201
  209.6 0.8 broadcast_in_dim.974
  212.2 1.4 fusion.95
  215.8 0.8 fusion.185
  220.3 37.0 %all_gather.54 = f32[16,8,320]{2,1,0:T(8,128)S(1)} all-gather(f32[1,8,320]{2,1,0:T(8,128)S(1)} %pad_maximum_fusion.22), channel_id=1, replica_groups=mesh['tiles'=16,'depth'=2] {'tiles'}, dimensions={0}, use_global_device_ids=true | all-gather | bytes 174080 | tf_op jit(solution)/shard_map/all_gather | solution.py:202
  260.6 38.1 %all_gather.55 = f32[16,8,320]{2,1,0:T(8,128)S(1)} all-gather(f32[1,8,320]{2,1,0:T(8,128)S(1)} %pad_maximum_fusion.23), channel_id=1, replica_groups=mesh['tiles'=16,'depth'=2] {'tiles'}, dimensions={0}, use_global_device_ids=true | all-gather | bytes 174080 | tf_op jit(solution)/shard_map/all_gather | solution.py:201
  299.1 0.8 broadcast_in_dim.968
  300.3 0.8 broadcast_in_dim.966
  302.3 1.5 fusion.86
  304.8 1.8 all_gather.56
  307.5 36.9 %all_gather.53 = f32[16,8,320]{2,1,0:T(8,128)S(1)} all-gather(f32[1,8,320]{2,1,0:T(8,128)S(1)} %pad_maximum_fusion.21), channel_id=1, replica_groups=mesh['tiles'=16,'depth'=2] {'tiles'}, dimensions={0}, use_global_device_ids=true | all-gather | bytes 174080 | tf_op jit(solution)/shard_map/all_gather | solution.py:200
  348.7 1.8 all_gather.59
  352.8 1.8 all_gather.46
  356.6 14.8 %rev.214 = f32[1,8,6300]{2,1,0:T(8,128)} reverse(f32[1,8,6300]{2,1,0:T(8,128)S(1)} %reduce_window_sum.27), dimensions={1} | reverse | bytes 403200 | tf_op jit(solution)/shard_map/jit(_flip)/rev | solution.py:207
  373.0 0.8 broadcast_in_dim.962
  373.9 0.8 broadcast_in_dim.964
  374.9 0.8 broadcast_in_dim.958
  375.9 0.8 broadcast_in_dim.960
  380.1 1.4 pad_maximum_fusion.12
  381.5 1.3 constant_dynamic-update-slice_fusion.3
  383.6 1.6 broadcast_multiply_fusion.2
  390.3 1.0 fusion.173
  391.3 0.8 fusion.212
  393.0 38.8 %all_gather.57 = f32[16,8,320]{2,1,0:T(8,128)S(1)} all-gather(f32[1,8,320]{2,1,0:T(8,128)S(1)} %pad_maximum_fusion.24), channel_id=1, replica_groups=mesh['tiles'=16,'depth'=2] {'tiles'}, dimensions={0}, use_global_device_ids=true | all-gather | bytes 174080 | tf_op jit(solution)/shard_map/all_gather | solution.py:202
  433.9 1.4 collective-permute-start.14
  435.4 1.3 collective-permute-start.15
  436.7 0.8 pad_maximum_fusion.10
  437.6 1.3 constant_dynamic-update-slice_fusion.2
  439.6 2.0 fusion.4
  442.0 0.8 pad_maximum_fusion.8
  442.9 8.5 %collective-permute-done.3 = f32[8,8,320]{2,1,0:T(8,128)S(1)} collective-permute-done((f32[8,8,320]{2,1,0:T(8,128)S(1)}, f32[8,8,320]{2,1,0:T(8,128)S(1)}, u32[]{:S(2)}, u32[]{:S(2)}) %collective-permute-start.3) | collective-permute-done | bytes 81952 | tf_op jit(solution)/shard_map/ppermute | solution.py:19
  455.5 1.1 broadcast_multiply_fusion.7
  457.1 1.8 all_gather.49
  461.2 36.9 %all_gather.51 = f32[16,8,320]{2,1,0:T(8,128)S(1)} all-gather(f32[1,8,320]{2,1,0:T(8,128)S(1)} %pad_maximum_fusion.19), channel_id=1, replica_groups=mesh['tiles'=16,'depth'=2] {'tiles'}, dimensions={0}, use_global_device_ids=true | all-gather | bytes 174080 | tf_op jit(solution)/shard_map/all_gather | solution.py:177
  499.1 38.0 %all_gather.47 = f32[16,8,320]{2,1,0:T(8,128)S(1)} all-gather(f32[1,8,320]{2,1,0:T(8,128)S(1)} %pad_maximum_fusion.15), channel_id=1, replica_groups=mesh['tiles'=16,'depth'=2] {'tiles'}, dimensions={0}, use_global_device_ids=true | all-gather | bytes 174080 | tf_op jit(solution)/shard_map/all_gather | solution.py:178
  538.2 37.0 %all_gather.50 = f32[16,8,320]{2,1,0:T(8,128)S(1)} all-gather(f32[1,8,320]{2,1,0:T(8,128)S(1)} %pad_maximum_fusion.18), channel_id=1, replica_groups=mesh['tiles'=16,'depth'=2] {'tiles'}, dimensions={0}, use_global_device_ids=true | all-gather | bytes 174080 | tf_op jit(solution)/shard_map/all_gather | solution.py:178
  578.7 0.8 fusion.203
  584.0 0.8 fusion.193
  584.8 1.9 collective-permute-start.10
  586.7 1.3 collective-permute-start.11
  588.8 0.8 broadcast_in_dim.924
  589.8 0.8 broadcast_in_dim.927
  590.7 0.8 broadcast_in_dim.934
  591.7 0.8 broadcast_in_dim.936
  592.7 0.8 broadcast_in_dim.950
  593.6 0.8 broadcast_in_dim.952
  596.0 3.2 fusion.19
  600.0 1.6 collective-permute-start.4
  602.1 1.5 collective-permute-done.4
  603.9 3.7 collective-permute-done.5
  607.7 4.1 collective-permute-done.6
  611.9 5.9 collective-permute-done.7
  621.0 1.1 fusion.48
  (625 shorter events, 88.2 us)
Async XLA Ops:
  1.4 7.8 %copy-start.3 = (f32[1,8,6300]{2,1,0:T(8,128)S(1)}, f32[1,8,6300]{2,1,0:T(8,128)}, u32[]{:S(2)}) copy-start(f32[1,8,6300]{2,1,0:T(8,128)} %param.26) | copy-start | bytes 604804
  6.7 5.6 copy-start.31
  103.6 43.9 %copy-start.6 = (f32[1,8,6300]{2,1,0:T(8,128)S(1)}, f32[1,8,6300]{2,1,0:T(8,128)}, u32[]{:S(2)}) copy-start(f32[1,8,6300]{2,1,0:T(8,128)} %param.35) | copy-start | bytes 604804
  104.0 43.5 %copy-start.5 = (f32[1,8,6300]{2,1,0:T(8,128)S(1)}, f32[1,8,6300]{2,1,0:T(8,128)}, u32[]{:S(2)}) copy-start(f32[1,8,6300]{2,1,0:T(8,128)} %param.34) | copy-start | bytes 604804
  143.3 4.2 copy-start.2
  143.9 3.5 copy-start.1
  144.0 3.5 copy-start
  147.5 5.2 copy-start.4
  149.5 233.4 %collective-permute-start.12 = (f32[1,1,6300]{2,1,0:T(1,128)}, f32[1,1,6300]{2,1,0:T(1,128)}, u32[]{:S(2)}, u32[]{:S(2)}) collective-permute-start(f32[1,1,6300]{2,1,0:T(1,128)} %get-tuple-element.277), channel_id=1, source_target_pairs={{0,1},{2,3},{4,5},{6,7},{8,9},{10,11},{12,13},{14,15},{16,17},{18,... | collective-permute-start | bytes 75608 | tf_op jit(solution)/shard_map/ppermute | solution.py:35
  151.4 231.5 %collective-permute-start.13 = (f32[1,1,6300]{2,1,0:T(1,128)}, f32[1,1,6300]{2,1,0:T(1,128)}, u32[]{:S(2)}, u32[]{:S(2)}) collective-permute-start(f32[1,1,6300]{2,1,0:T(1,128)} %get-tuple-element.278), channel_id=1, source_target_pairs={{1,0},{3,2},{5,4},{7,6},{9,8},{11,10},{13,12},{15,14},{17,16},{19,... | collective-permute-start | bytes 75608 | tf_op jit(solution)/shard_map/ppermute | solution.py:38
  153.0 1.1 copy-start.35
  154.2 225.9 %collective-permute-start = (f32[1,8,320]{2,1,0:T(8,128)}, f32[1,8,320]{2,1,0:T(8,128)}, u32[]{:S(2)}, u32[]{:S(2)}) collective-permute-start(f32[1,8,320]{2,1,0:T(8,128)} %get-tuple-element.240), channel_id=1, source_target_pairs={{0,30},{2,0},{4,2},{6,4},{8,6},{10,8},{12,10},{14,12},{16,14},{18,... | collective-permute-start | bytes 30728 | tf_op jit(solution)/shard_map/ppermute | solution.py:19
  154.8 299.8 %collective-permute-start.8 = (f32[1,1,6300]{2,1,0:T(1,128)}, f32[1,1,6300]{2,1,0:T(1,128)}, u32[]{:S(2)}, u32[]{:S(2)}) collective-permute-start(f32[1,1,6300]{2,1,0:T(1,128)} %get-tuple-element.354), channel_id=1, source_target_pairs={{0,1},{2,3},{4,5},{6,7},{8,9},{10,11},{12,13},{14,15},{16,17},{18,... | collective-permute-start | bytes 75608 | tf_op jit(solution)/shard_map/ppermute | solution.py:35
  159.0 295.6 %collective-permute-start.9 = (f32[1,1,6300]{2,1,0:T(1,128)}, f32[1,1,6300]{2,1,0:T(1,128)}, u32[]{:S(2)}, u32[]{:S(2)}) collective-permute-start(f32[1,1,6300]{2,1,0:T(1,128)} %get-tuple-element.355), channel_id=1, source_target_pairs={{1,0},{3,2},{5,4},{7,6},{9,8},{11,10},{13,12},{15,14},{17,16},{19,... | collective-permute-start | bytes 75608 | tf_op jit(solution)/shard_map/ppermute | solution.py:38
  300.3 1.3 copy-start.12
  350.6 1.3 copy-start.44
  375.9 2.2 copy-start.95
  375.9 2.9 copy-start.96
  375.9 4.2 copy-start.36
  375.9 4.2 copy-start.39
  375.9 4.2 copy-start.42
  376.8 6.1 copy-start.7
  381.5 1.4 copy-start.29
  381.5 55.1 %collective-permute-start.1 = (f32[2,8,320]{2,1,0:T(8,128)}, f32[2,8,320]{2,1,0:T(8,128)}, u32[]{:S(2)}, u32[]{:S(2)}) collective-permute-start(f32[2,8,320]{2,1,0:T(8,128)} %pad_maximum_fusion.12), channel_id=1, source_target_pairs={{0,28},{2,30},{4,0},{6,2},{8,4},{10,6},{12,8},{14,10},{16,12},{18,... | collective-permute-start | bytes 61448 | tf_op jit(solution)/shard_map/ppermute | solution.py:19
  388.1 1.5 copy-start.10
  388.1 1.5 copy-start.11
  388.1 1.5 copy-start.15
  388.1 1.5 copy-start.16
  388.1 1.5 copy-start.60
  433.7 2.9 copy-start.34
  433.7 2.9 copy-start.37
  433.8 2.9 copy-start.40
  433.8 2.9 copy-start.43
  433.8 5.2 copy-start.8
  433.8 5.2 copy-start.9
  433.9 5.0 collective-permute-start.14
  435.4 3.5 collective-permute-start.15
  437.5 1.4 copy-start.28
  437.5 4.5 collective-permute-start.2
  441.7 1.2 copy-start.27
  442.8 8.5 %collective-permute-start.3 = (f32[8,8,320]{2,1,0:T(8,128)S(1)}, f32[8,8,320]{2,1,0:T(8,128)S(1)}, u32[]{:S(2)}, u32[]{:S(2)}) collective-permute-start(f32[8,8,320]{2,1,0:T(8,128)S(1)} %pad_maximum_fusion.8), channel_id=1, source_target_pairs={{0,16},{2,18},{4,20},{6,22},{8,24},{10,26},{12,28},{14,30},{16,0},... | collective-permute-start | bytes 245768 | tf_op jit(solution)/shard_map/ppermute | solution.py:19
  454.4 1.0 copy-start.20
  584.8 10.4 %collective-permute-start.10 = (f32[1,1,6300]{2,1,0:T(1,128)}, f32[1,1,6300]{2,1,0:T(1,128)}, u32[]{:S(2)}, u32[]{:S(2)}) collective-permute-start(f32[1,1,6300]{2,1,0:T(1,128)} %get-tuple-element.344), channel_id=1, source_target_pairs={{0,1},{2,3},{4,5},{6,7},{8,9},{10,11},{12,13},{14,15},{16,17},{18,... | collective-permute-start | bytes 75608 | tf_op jit(solution)/shard_map/ppermute | solution.py:35
  586.7 8.5 %collective-permute-start.11 = (f32[1,1,6300]{2,1,0:T(1,128)}, f32[1,1,6300]{2,1,0:T(1,128)}, u32[]{:S(2)}, u32[]{:S(2)}) collective-permute-start(f32[1,1,6300]{2,1,0:T(1,128)} %get-tuple-element.345), channel_id=1, source_target_pairs={{1,0},{3,2},{5,4},{7,6},{9,8},{11,10},{13,12},{15,14},{17,16},{19,... | collective-permute-start | bytes 75608 | tf_op jit(solution)/shard_map/ppermute | solution.py:38
  594.9 1.0 copy-start.14
  594.9 1.0 copy-start.24
  594.9 1.0 copy-start.73
  594.9 1.0 copy-start.74
  594.9 1.0 copy-start.75
  594.9 1.0 copy-start.76
  594.9 1.0 copy-start.77
  595.0 1.0 copy-start.78
  595.0 1.0 copy-start.79
  595.0 1.0 copy-start.82
  595.0 1.0 copy-start.83
  600.0 3.7 collective-permute-start.4
  603.8 3.8 collective-permute-start.5
  607.7 4.1 collective-permute-start.6
  611.8 5.9 collective-permute-start.7
  619.9 1.0 copy-start.18
  619.9 1.0 copy-start.26
  619.9 1.0 copy-start.61
  619.9 1.0 copy-start.62
  620.0 1.0 copy-start.63
  (78 other events, 55.9 us)
